TPU v7x, 128 devices: a whole 4x4x4 slice. The times are simulated.
128 devices in a mesh: slab: 16 (over y, x), grp: 8 (over z, core).
Axes of the slice: x: 4, y: 4, z: 4, core: 2. Of those that a mesh axis runs over, the one named last changes fastest.
Arguments:
- initial: float32 [32, 64, 32, 256], P('grp', 'slab'), may hold values from 0 to 1
- target: float32 [32, 64, 32, 256], P('grp', 'slab'), may hold values from 0 to 0.6
- birth_step: int32 [64, 32, 256], P('slab'), may hold values from 0 to 4, as said below
- classes: int32 [32], P('grp'), may hold values from 0 to 3
- mobility: float32 [4, 4], replicated, may hold values from 0.2 to 2
Outputs:
- final_state: float32 [32, 64, 32, 256], P('grp', 'slab')
- initial_grad: float32 [32, 64, 32, 256], P('grp', 'slab')
- mobility_grad: float32 [4, 4], replicated
Inputs may be any that keep to these rules, and one draw needn't show every extreme that they name: A voxel takes part in step n when birth_step <= n; the value 4 means that it never takes part in the window; exactly one voxel has the value 0.
All inputs are finite; a program needn't handle non-finite values.
Results may differ from a plain program's by a relative error of at most 0.0001.
Values sent between devices are 32-bit elements; how exact they have to be, the bound alone decides.
No kernel may reach another device: no remote copies, remote signals or barrier semaphores. Data moves between devices by JAX's collectives and lax.ppermute only.
A program may use at most 64 MiB of HBM per device.

v0:
```python
import jax
import jax.numpy as jnp
from jax import lax
from jax.sharding import PartitionSpec as P

STEPS = 4
coupling = 0.3
stiffness = 1.0
time_step = 0.06


def extended_2(cells, sides, width):
    for axis, dim in sides:
        count = lax.axis_size(axis)
        ends = count - 1
        head = lax.slice_in_dim(cells, 0, width, axis=dim)
        tail = lax.slice_in_dim(cells, cells.shape[dim] - width, cells.shape[dim], axis=dim)
        cells = jnp.concatenate(
            [
                lax.ppermute(tail, axis, [(i, (i + 1) % count) for i in range(ends)]),
                cells,
                lax.ppermute(head, axis, [((i + 1) % count, i) for i in range(ends)]),
            ],
            axis=dim,
        )
    return cells


def laplace_local(extended):
    padded = jnp.pad(extended, ((0, 0), (0, 0), (1, 1), (1, 1)))
    centre = padded[:, 1:-1, 1:-1, 1:-1]
    return (
        padded[:, 2:, 1:-1, 1:-1]
        + padded[:, :-2, 1:-1, 1:-1]
        + padded[:, 1:-1, 2:, 1:-1]
        + padded[:, 1:-1, :-2, 1:-1]
        + padded[:, 1:-1, 1:-1, 2:]
        + padded[:, 1:-1, 1:-1, :-2]
        - 6.0 * centre
    )


def advance_local(fields, pair_rates, member, active):
    squared = fields * fields
    partial_sums = jnp.einsum("pk,pxzy->kxzy", member, squared, precision=lax.Precision.HIGHEST)
    class_sums = lax.psum(partial_sums, "grp")
    summed = jnp.sum(class_sums, axis=0)
    inverse = 1.0 / (1.0 + summed)
    driving = jnp.einsum("pk,kxzy->pxzy", pair_rates, class_sums, precision=lax.Precision.HIGHEST)
    rates = driving * inverse[None]
    extended = extended_2(fields, (("slab", 1),), 1)
    potential = (
        -fields
        + fields * squared
        + 2.0 * coupling * fields * (summed[None] - squared)
        - stiffness * laplace_local(extended)
    )
    weighted = active[None] * rates
    numerator, raw_denominator = lax.psum(
        (jnp.sum(weighted * potential, axis=(1, 2, 3)), jnp.sum(weighted, axis=(1, 2, 3))), "slab"
    )
    lagrange = numerator / jnp.maximum(raw_denominator, 1.0)
    updated = fields - time_step * weighted * (potential - lagrange[:, None, None, None])
    return (updated, potential, class_sums, numerator, raw_denominator)


def retreat(
    state_adj_next,
    fields,
    potential,
    class_sums,
    numerator,
    raw_denominator,
    member,
    pair_rates,
    active,
):
    squared = fields * fields
    summed = jnp.sum(class_sums, axis=0)
    inverse = 1.0 / (1.0 + summed)
    driving = jnp.einsum("pk,kxzy->pxzy", pair_rates, class_sums, precision=lax.Precision.HIGHEST)
    rates = driving * inverse[None]
    weighted = active[None] * rates
    denominator = jnp.maximum(raw_denominator, 1.0)
    lagrange = numerator / denominator
    scaled = time_step * active[None] * state_adj_next
    first_part = scaled * rates
    lagrange_adj = lax.psum(jnp.sum(first_part, axis=(1, 2, 3)), "slab")
    numer_adj = lagrange_adj / denominator
    potential_adj = weighted * numer_adj[:, None, None, None] - first_part
    extended = extended_2(potential_adj, (("slab", 1),), 1)
    curvature = laplace_local(extended)
    denom_adj = jnp.where(
        raw_denominator > 1.0, -lagrange_adj * numerator / (denominator * denominator), 0.0
    )
    rate_adj = -scaled * (potential - lagrange[:, None, None, None]) + active[None] * (
        numer_adj[:, None, None, None] * potential + denom_adj[:, None, None, None]
    )
    drive_adj = rate_adj * inverse[None]
    state_adj = (
        state_adj_next
        + potential_adj
        * (
            -1.0
            + 3.0 * squared
            + 2.0 * coupling * (summed[None] - squared)
            - 4.0 * coupling * squared
        )
        - stiffness * curvature
    )
    weighted_sums = jnp.einsum(
        "pk,pxzy->kxzy", pair_rates, drive_adj, precision=lax.Precision.HIGHEST
    )
    shared_sum = jnp.sum(
        2.0 * coupling * potential_adj * fields - (inverse * inverse)[None] * rate_adj * driving,
        axis=0,
    )
    weighted_sums, shared_sum = lax.psum((weighted_sums, shared_sum), "grp")
    class_adj = weighted_sums + shared_sum[None]
    state_adj = state_adj + 2.0 * fields * jnp.einsum(
        "pk,kxzy->pxzy", member, class_adj, precision=lax.Precision.HIGHEST
    )
    products = jnp.einsum("pxzy,kxzy->pk", drive_adj, class_sums, precision=lax.Precision.HIGHEST)
    mobility_term = jnp.dot(member.T, products, precision=lax.Precision.HIGHEST)
    return (state_adj, mobility_term)


def on_device(initial, target, birth_step, classes, mobility):
    classes_count = mobility.shape[0]
    member = (classes[:, None] == jnp.arange(classes_count, dtype=jnp.int32)[None, :]).astype(
        jnp.float32
    )
    pair_rates = jnp.dot(member, mobility, precision=lax.Precision.HIGHEST)
    fields = initial
    stored = []
    for step_index in range(STEPS):
        active = (birth_step <= step_index).astype(jnp.float32)
        updated, potential, class_sums, numerator, raw_denominator = advance_local(
            fields, pair_rates, member, active
        )
        stored.append((fields, potential, class_sums, numerator, raw_denominator, active))
        fields = updated
    state_adj = fields - target
    mobility_acc = jnp.zeros((classes_count, classes_count), jnp.float32)
    for step_index in range(STEPS - 1, -1, -1):
        saved_fields, potential, class_sums, numerator, raw_denominator, active = stored[step_index]
        state_adj, mobility_term = retreat(
            state_adj,
            saved_fields,
            potential,
            class_sums,
            numerator,
            raw_denominator,
            member,
            pair_rates,
            active,
        )
        mobility_acc = mobility_acc + mobility_term
    mobility_total = lax.psum(mobility_acc, ("slab", "grp"))
    scale = time_step * (initial.shape[1] * lax.axis_size("slab")) * initial.shape[2]
    return (fields, state_adj, mobility_total / scale)


def solution(mesh):
    return jax.shard_map(
        on_device,
        mesh=mesh,
        in_specs=(
            P("grp", "slab", None, None),
            P("grp", "slab", None, None),
            P("slab", None, None),
            P("grp"),
            P(),
        ),
        out_specs=(P("grp", "slab", None, None), P("grp", "slab", None, None), P()),
        check_vma=False,
    )
```

profile of v0, /device:TPU:0, one launch (start us, length us, event | category | flops | bytes accessed | tf_op | source)
XLA Modules:
  0.0 990.1 jit_solution(4415834130746513272)
XLA Ops:
  7.2 1.4 copy.20
  8.7 3.6 collective-permute-start.1
  13.7 1.8 fusion.9
  20.0 60.5 %all-reduce.25.cloned.1.call-done = f32[4,4,32,256]{3,0,2,1:T(4,128)} async-done(((f32[4,4,32,256]{3,0,2,1:T(4,128)}), f32[4,4,32,256]{3,0,2,1:T(4,128)}) %all-reduce.25.cloned.1.call-update) | async-done | bytes 524304 | tf_op jit(solution)/shard_map/psum | solution.py:46
  80.5 1.4 reduce_sum.196
  82.6 3.1 fusion.134
  85.7 40.3 %all-reduce.11 = (f32[4]{0:T(128)S(1)}, f32[4]{0:T(128)S(1)}) all-reduce(f32[4]{0:T(128)S(1)} %get-tuple-element.13, f32[4]{0:T(128)S(1)} %get-tuple-element.12), channel_id=1, replica_groups=mesh['slab'=16,'grp'=8] {'slab'}, use_global_device_ids=true, to_apply=%region_3.4 | all-reduce | flops 8 | bytes 64 | tf_op jit(solution)/shard_map/psum | solution.py:59
  126.6 1.7 multiply_subtract_fusion.11
  130.9 1.6 fusion.7
  132.6 3.9 collective-permute-done.2
  136.5 1.8 select_maximum_fusion.12
  138.2 52.1 %all-reduce.27.cloned.1.call-done = f32[4,4,32,256]{3,0,2,1:T(4,128)} async-done(((f32[4,4,32,256]{3,0,2,1:T(4,128)}), f32[4,4,32,256]{3,0,2,1:T(4,128)}) %all-reduce.27.cloned.1.call-update) | async-done | bytes 524304 | tf_op jit(solution)/shard_map/psum | solution.py:46
  190.3 1.4 reduce_sum.199
  192.4 4.1 fusion.135
  196.5 40.3 %all-reduce.10 = (f32[4]{0:T(128)S(1)}, f32[4]{0:T(128)S(1)}) all-reduce(f32[4]{0:T(128)S(1)} %get-tuple-element.11, f32[4]{0:T(128)S(1)} %get-tuple-element.10), channel_id=1, replica_groups=mesh['slab'=16,'grp'=8] {'slab'}, use_global_device_ids=true, to_apply=%region_9.10 | all-reduce | flops 8 | bytes 64 | tf_op jit(solution)/shard_map/psum | solution.py:59
  240.4 1.6 fusion.5
  242.2 3.7 collective-permute-done.4
  245.9 1.8 select_maximum_fusion.10
  247.7 52.0 %all-reduce.29.cloned.1.call-done = f32[4,4,32,256]{3,0,2,1:T(4,128)} async-done(((f32[4,4,32,256]{3,0,2,1:T(4,128)}), f32[4,4,32,256]{3,0,2,1:T(4,128)}) %all-reduce.29.cloned.1.call-update) | async-done | bytes 524304 | tf_op jit(solution)/shard_map/psum | solution.py:46
  299.7 1.4 reduce_sum.202
  301.8 4.6 fusion.136
  306.4 40.4 %all-reduce.9 = (f32[4]{0:T(128)S(1)}, f32[4]{0:T(128)S(1)}) all-reduce(f32[4]{0:T(128)} %get-tuple-element.9, f32[4]{0:T(128)} %get-tuple-element.8), channel_id=1, replica_groups=mesh['slab'=16,'grp'=8] {'slab'}, use_global_device_ids=true, to_apply=%region_15.16 | all-reduce | flops 8 | bytes 64 | tf_op jit(solution)/shard_map/psum | solution.py:59
  352.0 1.6 fusion.3
  353.7 4.0 collective-permute-done.6
  357.7 1.8 select_maximum_fusion.8
  359.5 51.8 %all-reduce.31.cloned.1.call-done = f32[4,4,32,256]{3,0,2,1:T(4,128)} async-done(((f32[4,4,32,256]{3,0,2,1:T(4,128)}), f32[4,4,32,256]{3,0,2,1:T(4,128)}) %all-reduce.31.cloned.1.call-update) | async-done | bytes 524304 | tf_op jit(solution)/shard_map/psum | solution.py:46
  411.3 1.4 reduce_sum.205
  413.4 5.4 fusion.137
  418.8 40.4 %all-reduce.8 = (f32[4]{0:T(128)S(1)}, f32[4]{0:T(128)S(1)}) all-reduce(f32[4]{0:T(128)} %get-tuple-element.7, f32[4]{0:T(128)} %get-tuple-element.6), channel_id=1, replica_groups=mesh['slab'=16,'grp'=8] {'slab'}, use_global_device_ids=true, to_apply=%region_21.22 | all-reduce | flops 8 | bytes 64 | tf_op jit(solution)/shard_map/psum | solution.py:59
  459.3 3.1 fusion.126
  462.4 35.5 %psum.187 = f32[4]{0:T(128)S(1)} all-reduce(f32[4]{0:T(128)S(1)} %get-tuple-element.48), channel_id=1, replica_groups=mesh['slab'=16,'grp'=8] {'slab'}, use_global_device_ids=true, to_apply=%region_25.26 | all-reduce | flops 4 | bytes 32 | tf_op jit(solution)/shard_map/psum | solution.py:88
  497.9 3.3 subtract_reduce_fusion.3
  501.9 4.5 collective-permute-start.9
  507.7 2.0 fusion.87
  511.0 3.6 convolution_bitcast_fusion.3
  515.5 2.7 select_maximum_fusion.6
  518.2 50.4 %all-reduce.39.cloned.1.call-done = (f32[4,4,32,256]{3,0,2,1:T(4,128)}, f32[4,32,256]{2,1,0:T(8,128)}) async-done(((f32[4,4,32,256]{3,0,2,1:T(4,128)}, f32[4,32,256]{2,1,0:T(8,128)}), (f32[4,4,32,256]{3,0,2,1:T(4,128)}, f32[4,32,256]{2,1,0:T(8,128)})) %all-reduce.39.cloned.1.call-update) | async-done | bytes 655376 | tf_op jit(solution)/shard_map/psum | solution.py:118
  568.6 6.0 fusion.127
  574.6 40.4 %psum.190 = f32[4]{0:T(128)S(1)} all-reduce(f32[4]{0:T(128)} %get-tuple-element.99), channel_id=1, replica_groups=mesh['slab'=16,'grp'=8] {'slab'}, use_global_device_ids=true, to_apply=%region_30.31 | all-reduce | flops 4 | bytes 32 | tf_op jit(solution)/shard_map/psum | solution.py:88
  615.7 3.0 subtract_reduce_fusion.2
  619.5 1.9 collective-permute-start.11
  622.7 2.0 fusion.84
  624.8 2.5 convolution_bitcast_fusion.2
  627.3 1.6 convolution_add_fusion.2
  628.9 2.7 select_maximum_fusion.4
  631.7 51.4 %all-reduce.37.cloned.1.call-done = (f32[4,4,32,256]{3,0,2,1:T(4,128)}, f32[4,32,256]{2,1,0:T(8,128)}) async-done(((f32[4,4,32,256]{3,0,2,1:T(4,128)}, f32[4,32,256]{2,1,0:T(8,128)}), (f32[4,4,32,256]{3,0,2,1:T(4,128)}, f32[4,32,256]{2,1,0:T(8,128)})) %all-reduce.37.cloned.1.call-update) | async-done | bytes 655376 | tf_op jit(solution)/shard_map/psum | solution.py:118
  683.1 5.8 fusion.128
  688.9 40.8 %psum.193 = f32[4]{0:T(128)S(1)} all-reduce(f32[4]{0:T(128)} %get-tuple-element.101), channel_id=1, replica_groups=mesh['slab'=16,'grp'=8] {'slab'}, use_global_device_ids=true, to_apply=%region_35.36 | all-reduce | flops 4 | bytes 32 | tf_op jit(solution)/shard_map/psum | solution.py:88
  730.3 2.9 subtract_reduce_fusion.1
  733.2 1.4 collective-permute-start.13
  736.0 2.0 fusion.81
  738.1 2.5 convolution_bitcast_fusion.1
  740.6 1.6 convolution_add_fusion.1
  742.2 1.8 select_maximum_fusion.2
  744.0 52.3 %all-reduce.35.cloned.1.call-done = (f32[4,4,32,256]{3,0,2,1:T(4,128)}, f32[4,32,256]{2,1,0:T(8,128)}) async-done(((f32[4,4,32,256]{3,0,2,1:T(4,128)}, f32[4,32,256]{2,1,0:T(8,128)}), (f32[4,4,32,256]{3,0,2,1:T(4,128)}, f32[4,32,256]{2,1,0:T(8,128)})) %all-reduce.35.cloned.1.call-update) | async-done | bytes 655376 | tf_op jit(solution)/shard_map/psum | solution.py:118
  796.3 5.8 fusion.129
  802.1 40.4 %psum.196 = f32[4]{0:T(128)S(1)} all-reduce(f32[4]{0:T(128)} %get-tuple-element.103), channel_id=1, replica_groups=mesh['slab'=16,'grp'=8] {'slab'}, use_global_device_ids=true, to_apply=%region_40.41 | all-reduce | flops 4 | bytes 32 | tf_op jit(solution)/shard_map/psum | solution.py:88
  843.3 3.0 subtract_reduce_fusion
  846.3 2.5 convolution_bitcast_fusion
  849.1 2.0 fusion.78
  851.1 62.5 %psum.199 = f32[4,4]{1,0:T(4,128)S(1)} all-reduce(f32[4,4]{1,0:T(4,128)S(1)} %convolution_add_fusion), channel_id=1, replica_groups=mesh['slab'=16,'grp'=8] {'slab','grp'}, use_global_device_ids=true, to_apply=%region_44.45 | all-reduce | flops 16 | bytes 128 | tf_op jit(solution)/shard_map/psum | solution.py:159
  917.6 4.4 collective-permute-done.14
  922.6 56.6 %all-reduce.33.cloned.1.call-done = (f32[4,4,32,256]{3,0,2,1:T(4,128)}, f32[4,32,256]{2,1,0:T(8,128)}) async-done(((f32[4,4,32,256]{3,0,2,1:T(4,128)}, f32[4,32,256]{2,1,0:T(8,128)}), (f32[4,4,32,256]{3,0,2,1:T(4,128)}, f32[4,32,256]{2,1,0:T(8,128)})) %all-reduce.33.cloned.1.call-update) | async-done | bytes 655376 | tf_op jit(solution)/shard_map/psum | solution.py:118
  979.2 3.0 fusion.20
  (177 shorter events, 36.1 us)
Async XLA Ops:
  7.2 12.0 %copy-start = (f32[4,4]{1,0:T(4,128)S(1)}, f32[4,4]{1,0:T(4,128)}, u32[]{:S(2)}) copy-start(f32[4,4]{1,0:T(4,128)} %param.9) | copy-start | bytes 196
  7.2 6.5 copy-start.1
  7.2 6.5 copy-start.40
  7.2 73.3 %all-reduce.25.cloned.1.call-start = ((), (), s32[]{:S(2)}) async-start(), calls=%async_computation | async-start | bytes 1048576 | tf_op jit(solution)/shard_map/psum | solution.py:46
  8.7 6.9 copy-start.39
  8.7 10.6 %collective-permute-start.1 = (f32[4,1,32,256]{3,0,2,1:T(4,128)S(1)}, f32[4,1,32,256]{3,0,2,1:T(4,128)S(1)}, u32[]{:S(2)}, u32[]{:S(2)}) collective-permute-start(f32[4,1,32,256]{3,0,2,1:T(4,128)S(1)} %get-tuple-element.71), channel_id=1, source_target_pairs={{0,8},{8,16},{16,24},{24,32},{32,40},{40,48},{48,56},{56,64},{64,7... | collective-permute-start | bytes 393224 | tf_op jit(solution)/shard_map/ppermute | solution.py:20
  12.4 7.0 collective-permute-start
  15.5 174.8 %all-reduce.27.cloned.1.call-start = ((), (), s32[]{:S(2)}) async-start(), calls=%async_computation.1 | async-start | bytes 1048576 | tf_op jit(solution)/shard_map/psum | solution.py:46
  19.3 61.2 %copy-start.35 = (f32[4,1,32,256]{3,0,2,1:T(4,128)}, f32[4,1,32,256]{3,0,2,1:T(4,128)S(1)}, u32[]{:S(2)}) copy-start(f32[4,1,32,256]{3,0,2,1:T(4,128)S(1)} %collective-permute-done.1) | copy-start | bytes 393220
  85.7 42.6 %copy-start.5 = (f32[4,4,32,256]{3,0,2,1:T(4,128)}, f32[4,4,32,256]{3,0,2,1:T(4,128)S(1)}, u32[]{:S(2)}) copy-start(f32[4,4,32,256]{3,0,2,1:T(4,128)S(1)} %get-tuple-element.56) | copy-start | bytes 1572868
  85.7 42.6 %copy-start.7 = (f32[4,4,32,256]{3,0,2,1:T(4,128)}, f32[4,4,32,256]{3,0,2,1:T(4,128)S(1)}, u32[]{:S(2)}) copy-start(f32[4,4,32,256]{3,0,2,1:T(4,128)S(1)} %get-tuple-element.95) | copy-start | bytes 1572868
  128.3 4.3 collective-permute-start.3
  129.6 6.9 collective-permute-start.2
  132.5 59.8 %copy-start.21 = (f32[4,32,256]{2,1,0:T(8,128)S(1)}, f32[4,32,256]{2,1,0:T(8,128)}, u32[]{:S(2)}) copy-start(f32[4,32,256]{2,1,0:T(8,128)} %convert_element_type.23) | copy-start | bytes 393220
  132.6 167.1 %all-reduce.29.cloned.1.call-start = ((), (), s32[]{:S(2)}) async-start(), calls=%async_computation.2 | async-start | bytes 1048576 | tf_op jit(solution)/shard_map/psum | solution.py:46
  191.7 4.8 copy-start.30
  196.5 41.3 %copy-start.10 = (f32[4,4,32,256]{3,0,2,1:T(4,128)}, f32[4,4,32,256]{3,0,2,1:T(4,128)S(1)}, u32[]{:S(2)}) copy-start(f32[4,4,32,256]{3,0,2,1:T(4,128)S(1)} %get-tuple-element.55) | copy-start | bytes 1572868
  196.5 41.3 %copy-start.12 = (f32[4,4,32,256]{3,0,2,1:T(4,128)}, f32[4,4,32,256]{3,0,2,1:T(4,128)S(1)}, u32[]{:S(2)}) copy-start(f32[4,4,32,256]{3,0,2,1:T(4,128)S(1)} %get-tuple-element.96) | copy-start | bytes 1572868
  237.8 4.5 collective-permute-start.5
  239.1 6.9 collective-permute-start.4
  242.0 59.8 %copy-start.22 = (f32[4,32,256]{2,1,0:T(8,128)S(1)}, f32[4,32,256]{2,1,0:T(8,128)}, u32[]{:S(2)}) copy-start(f32[4,32,256]{2,1,0:T(8,128)} %convert_element_type.24) | copy-start | bytes 393220
  242.0 169.3 %all-reduce.31.cloned.1.call-start = ((), (), s32[]{:S(2)}) async-start(), calls=%async_computation.3 | async-start | bytes 1048576 | tf_op jit(solution)/shard_map/psum | solution.py:46
  301.0 5.3 copy-start.32
  306.4 43.0 %copy-start.15 = (f32[4,4,32,256]{3,0,2,1:T(4,128)}, f32[4,4,32,256]{3,0,2,1:T(4,128)S(1)}, u32[]{:S(2)}) copy-start(f32[4,4,32,256]{3,0,2,1:T(4,128)S(1)} %get-tuple-element.54) | copy-start | bytes 1572868
  306.4 43.0 %copy-start.17 = (f32[4,4,32,256]{3,0,2,1:T(4,128)}, f32[4,4,32,256]{3,0,2,1:T(4,128)S(1)}, u32[]{:S(2)}) copy-start(f32[4,4,32,256]{3,0,2,1:T(4,128)S(1)} %get-tuple-element.97) | copy-start | bytes 1572868
  349.4 4.3 collective-permute-start.7
  350.7 7.1 collective-permute-start.6
  353.6 59.7 %copy-start.23 = (f32[4,32,256]{2,1,0:T(8,128)S(1)}, f32[4,32,256]{2,1,0:T(8,128)}, u32[]{:S(2)}) copy-start(f32[4,32,256]{2,1,0:T(8,128)} %convert_element_type.25) | copy-start | bytes 393220
  353.6 215.0 %all-reduce.39.cloned.1.call-start = ((), (), s32[]{:S(2)}) async-start(), calls=%async_computation.7 | async-start | bytes 1310720 | tf_op jit(solution)/shard_map/psum | solution.py:118
  353.7 57.6 %copy-start.37 = (f32[4,1,32,256]{3,0,2,1:T(4,128)}, f32[4,1,32,256]{3,0,2,1:T(4,128)S(1)}, u32[]{:S(2)}) copy-start(f32[4,1,32,256]{3,0,2,1:T(4,128)S(1)} %collective-permute-done.7) | copy-start | bytes 393220
  357.7 54.9 %copy-start.38 = (f32[4,1,32,256]{3,0,2,1:T(4,128)}, f32[4,1,32,256]{3,0,2,1:T(4,128)S(1)}, u32[]{:S(2)}) copy-start(f32[4,1,32,256]{3,0,2,1:T(4,128)S(1)} %collective-permute-done.6) | copy-start | bytes 393220
  412.7 6.1 copy-start.33
  413.4 45.9 %copy-start.2 = (f32[4,32,256]{2,1,0:T(8,128)}, f32[4,32,256]{2,1,0:T(8,128)S(1)}, u32[]{:S(2)}) copy-start(f32[4,32,256]{2,1,0:T(8,128)S(1)} %get-tuple-element.80) | copy-start | bytes 393220
  413.4 45.9 %copy-start.24 = (f32[4,32,256]{2,1,0:T(8,128)S(1)}, f32[4,32,256]{2,1,0:T(8,128)}, u32[]{:S(2)}) copy-start(f32[4,32,256]{2,1,0:T(8,128)} %get-tuple-element.51) | copy-start | bytes 393220
  418.8 43.6 %copy-start.19 = (f32[4,4,32,256]{3,0,2,1:T(4,128)}, f32[4,4,32,256]{3,0,2,1:T(4,128)S(1)}, u32[]{:S(2)}) copy-start(f32[4,4,32,256]{3,0,2,1:T(4,128)S(1)} %get-tuple-element.53) | copy-start | bytes 1572868
  459.2 3.1 copy-start.43
  497.9 9.8 copy-start.3
  501.2 8.6 copy-start.18
  501.9 13.6 %collective-permute-start.9 = (f32[4,1,32,256]{3,0,2,1:T(4,128)}, f32[4,1,32,256]{3,0,2,1:T(4,128)}, u32[]{:S(2)}, u32[]{:S(2)}) collective-permute-start(f32[4,1,32,256]{3,0,2,1:T(4,128)} %get-tuple-element.63), channel_id=1, source_target_pairs={{0,8},{8,16},{16,24},{24,32},{32,40},{40,48},{48,56},{56,64},{64,7... | collective-permute-start | bytes 393224 | tf_op jit(solution)/shard_map/ppermute | solution.py:20
  506.4 9.0 collective-permute-start.8
  510.7 172.4 %all-reduce.37.cloned.1.call-start = ((), (), s32[]{:S(2)}) async-start(), calls=%async_computation.6 | async-start | bytes 1310720 | tf_op jit(solution)/shard_map/psum | solution.py:118
  568.6 47.1 %copy-start.16 = (f32[4,4,32,256]{3,0,2,1:T(4,128)S(1)}, f32[4,4,32,256]{3,0,2,1:T(4,128)}, u32[]{:S(2)}) copy-start(f32[4,4,32,256]{3,0,2,1:T(4,128)} %copy-done.15) | copy-start | bytes 1572868
  618.7 6.1 copy-start.14
  619.5 9.5 collective-permute-start.11
  621.4 7.5 collective-permute-start.10
  624.8 171.5 %all-reduce.35.cloned.1.call-start = ((), (), s32[]{:S(2)}) async-start(), calls=%async_computation.5 | async-start | bytes 1310720 | tf_op jit(solution)/shard_map/psum | solution.py:118
  627.3 55.8 %copy-start.13 = (f32[4,4,32,256]{3,0,2,1:T(4,128)S(1)}, f32[4,4,32,256]{3,0,2,1:T(4,128)}, u32[]{:S(2)}) copy-start(f32[4,4,32,256]{3,0,2,1:T(4,128)} %copy-done.12) | copy-start | bytes 1572868
  627.3 55.8 %copy-start.29 = (f32[4,32,256]{2,1,0:T(8,128)S(1)}, f32[4,32,256]{2,1,0:T(8,128)}, u32[]{:S(2)}) copy-start(f32[4,32,256]{2,1,0:T(8,128)} %get-tuple-element.81) | copy-start | bytes 393220
  683.1 47.2 %copy-start.11 = (f32[4,4,32,256]{3,0,2,1:T(4,128)S(1)}, f32[4,4,32,256]{3,0,2,1:T(4,128)}, u32[]{:S(2)}) copy-start(f32[4,4,32,256]{3,0,2,1:T(4,128)} %copy-done.10) | copy-start | bytes 1572868
  733.2 4.9 copy-start.9
  733.2 9.0 collective-permute-start.13
  734.7 7.6 collective-permute-start.12
  738.0 241.2 %all-reduce.33.cloned.1.call-start = ((), (), s32[]{:S(2)}) async-start(), calls=%async_computation.4 | async-start | bytes 1310720 | tf_op jit(solution)/shard_map/psum | solution.py:118
  740.6 55.7 %copy-start.8 = (f32[4,4,32,256]{3,0,2,1:T(4,128)S(1)}, f32[4,4,32,256]{3,0,2,1:T(4,128)}, u32[]{:S(2)}) copy-start(f32[4,4,32,256]{3,0,2,1:T(4,128)} %copy-done.7) | copy-start | bytes 1572868
  740.6 55.7 %copy-start.28 = (f32[4,32,256]{2,1,0:T(8,128)S(1)}, f32[4,32,256]{2,1,0:T(8,128)}, u32[]{:S(2)}) copy-start(f32[4,32,256]{2,1,0:T(8,128)} %get-tuple-element.83) | copy-start | bytes 393220
  740.6 55.7 %copy-start.31 = (f32[4,32,256]{2,1,0:T(8,128)S(1)}, f32[4,32,256]{2,1,0:T(8,128)}, u32[]{:S(2)}) copy-start(f32[4,32,256]{2,1,0:T(8,128)} %copy-done.30) | copy-start | bytes 393220
  796.3 46.9 %copy-start.6 = (f32[4,4,32,256]{3,0,2,1:T(4,128)S(1)}, f32[4,4,32,256]{3,0,2,1:T(4,128)}, u32[]{:S(2)}) copy-start(f32[4,4,32,256]{3,0,2,1:T(4,128)} %copy-done.5) | copy-start | bytes 1572868
  796.3 46.9 %copy-start.20 = (f32[4,32,256]{2,1,0:T(8,128)S(1)}, f32[4,32,256]{2,1,0:T(8,128)}, u32[]{:S(2)}) copy-start(f32[4,32,256]{2,1,0:T(8,128)} %convert_element_type.22) | copy-start | bytes 393220
  796.3 46.9 %copy-start.25 = (f32[4,32,256]{2,1,0:T(8,128)S(1)}, f32[4,32,256]{2,1,0:T(8,128)}, u32[]{:S(2)}) copy-start(f32[4,32,256]{2,1,0:T(8,128)} %get-tuple-element.73) | copy-start | bytes 393220
  843.3 5.6 copy-start.50
  913.7 3.9 collective-permute-start.15
  915.0 7.0 collective-permute-start.14
  916.3 62.9 %copy-start.27 = (f32[4,32,256]{2,1,0:T(8,128)S(1)}, f32[4,32,256]{2,1,0:T(8,128)}, u32[]{:S(2)}) copy-start(f32[4,32,256]{2,1,0:T(8,128)} %copy-done.26) | copy-start | bytes 393220
  916.3 62.9 %copy-start.34 = (f32[4,4,32,256]{3,0,2,1:T(4,128)S(1)}, f32[4,4,32,256]{3,0,2,1:T(4,128)}, u32[]{:S(2)}) copy-start(f32[4,4,32,256]{3,0,2,1:T(4,128)} %get-tuple-element.104) | copy-start | bytes 1572868
  (11 other events, 10.8 us)
Sparse Core Ops, SparseCore 0:
  15.7 64.7 all-reduce.24
  132.7 57.5 all-reduce.26
  242.1 57.5 all-reduce.28
  353.7 57.5 all-reduce.30
  510.8 57.7 all-reduce.38
  624.9 58.1 all-reduce.36
  738.1 58.1 all-reduce.34
  916.5 62.6 all-reduce.32
where the time goes:
time: 999 us; the launch traced here: 990 us
  waiting for transfers between devices  444 us (44%)
  blocking collectives  381 us (38%)
  matrix products  68.3 us (7%)
  other arithmetic  46.8 us (5%)
  starting transfers between devices  27.8 us (3%)
  between operations  15 us (2%)
    psum x4, waiting for transfers between devices, advance_local(): class_sums = lax.psum(partial_sums, 'grp')  216 us
    psum x4, waiting for transfers between devices, retreat(): weighted_sums, shared_sum = lax.psum((weighted_sums, shared_sum), 'grp')  211 us
    psum x4, blocking collectives, advance_local(): lax.psum((jnp.sum(weighted * potential, axis=(1, 2, 3)), jnp.sum(weighted...  162 us
    psum x4, blocking collectives, retreat(): lagrange_adj = lax.psum(jnp.sum(first_part, axis=(1, 2, 3)), 'slab')  157 us
    psum x1, blocking collectives, on_device(): mobility_total = lax.psum(mobility_acc, ('slab', 'grp'))  62.5 us
    dot_general x4, matrix products, retreat(): jnp.einsum('pk,kxzy->pxzy', member, class_adj, precision=lax.Precision.HI...  20.6 us
  transfers between devices with their start and end apart: 24, of which 13 were waited for; matrix products, arithmetic and copies ran while one was open for 4% of the time, Pallas kernels for 0%

commit v1 on v0

--- a/solution.py
+++ b/solution.py
@@ -156,7 +156,7 @@
             active,
         )
         mobility_acc = mobility_acc + mobility_term
-    mobility_total = lax.psum(mobility_acc, ("slab", "grp"))
+    mobility_total = lax.psum(lax.psum(mobility_acc, "grp"), "slab")
     scale = time_step * (initial.shape[1] * lax.axis_size("slab")) * initial.shape[2]
     return (fields, state_adj, mobility_total / scale)
 

time: 999 us -> 984 us (0.985)
  blocking collectives: 381 us -> 367 us
    psum x1 -> x2, blocking collectives: 62.5 us -> 47.9 us  [on_device(): mobility_total = lax.psum(lax.psum(mobility_acc, 'grp'), 'slab')]
  transfers between devices with their start and end apart: 24 -> 24, of which waited for: 13 -> 14; matrix products, arithmetic and copies ran while one was open for 4% -> 5% of each run, Pallas kernels for 0% -> 0%
where the time goes in v1:
time: 984 us; the launch traced here: 975 us
  waiting for transfers between devices  439 us (45%)
  blocking collectives  367 us (37%)
  matrix products  70.1 us (7%)
  other arithmetic  45.5 us (5%)
  starting transfers between devices  30.4 us (3%)
  between operations  15 us (2%)
    psum x4, waiting for transfers between devices, advance_local(): class_sums = lax.psum(partial_sums, 'grp')  215 us
    psum x4, waiting for transfers between devices, retreat(): weighted_sums, shared_sum = lax.psum((weighted_sums, shared_sum), 'grp')  206 us
    psum x4, blocking collectives, advance_local(): lax.psum((jnp.sum(weighted * potential, axis=(1, 2, 3)), jnp.sum(weighted...  162 us
    psum x4, blocking collectives, retreat(): lagrange_adj = lax.psum(jnp.sum(first_part, axis=(1, 2, 3)), 'slab')  157 us
    psum x2, blocking collectives, on_device(): mobility_total = lax.psum(lax.psum(mobility_acc, 'grp'), 'slab')  47.9 us
    dot_general x4, matrix products, retreat(): jnp.einsum('pk,kxzy->pxzy', member, class_adj, precision=lax.Precision.HI...  21 us
  transfers between devices with their start and end apart: 24, of which 14 were waited for; matrix products, arithmetic and copies ran while one was open for 5% of the time, Pallas kernels for 0%

profile of v1, /device:TPU:0, one launch (start us, length us, event | category | flops | bytes accessed | tf_op | source)
XLA Modules:
  0.0 974.7 jit_solution(15163687642971807748)
XLA Ops:
  7.2 1.4 copy.20
  8.7 3.6 collective-permute-start.1
  13.7 1.8 fusion.9
  19.2 1.7 select_maximum_fusion.14
  21.0 59.5 %all-reduce.25.cloned.1.call-done = f32[4,4,32,256]{3,0,2,1:T(4,128)} async-done(((f32[4,4,32,256]{3,0,2,1:T(4,128)}), f32[4,4,32,256]{3,0,2,1:T(4,128)}) %all-reduce.25.cloned.1.call-update) | async-done | bytes 524304 | tf_op jit(solution)/shard_map/psum | solution.py:46
  80.5 1.4 reduce_sum.196
  82.5 4.2 fusion.134
  86.8 40.3 %all-reduce.11 = (f32[4]{0:T(128)S(1)}, f32[4]{0:T(128)S(1)}) all-reduce(f32[4]{0:T(128)S(1)} %get-tuple-element.13, f32[4]{0:T(128)S(1)} %get-tuple-element.12), channel_id=1, replica_groups=mesh['slab'=16,'grp'=8] {'slab'}, use_global_device_ids=true, to_apply=%region_3.4 | all-reduce | flops 8 | bytes 64 | tf_op jit(solution)/shard_map/psum | solution.py:59
  131.0 1.6 fusion.7
  132.7 3.9 collective-permute-done.2
  136.6 1.7 select_maximum_fusion.12
  138.3 52.0 %all-reduce.27.cloned.1.call-done = f32[4,4,32,256]{3,0,2,1:T(4,128)} async-done(((f32[4,4,32,256]{3,0,2,1:T(4,128)}), f32[4,4,32,256]{3,0,2,1:T(4,128)}) %all-reduce.27.cloned.1.call-update) | async-done | bytes 524304 | tf_op jit(solution)/shard_map/psum | solution.py:46
  192.4 4.2 fusion.135
  196.6 40.3 %all-reduce.10 = (f32[4]{0:T(128)S(1)}, f32[4]{0:T(128)S(1)}) all-reduce(f32[4]{0:T(128)S(1)} %get-tuple-element.11, f32[4]{0:T(128)S(1)} %get-tuple-element.10), channel_id=1, replica_groups=mesh['slab'=16,'grp'=8] {'slab'}, use_global_device_ids=true, to_apply=%region_9.10 | all-reduce | flops 8 | bytes 64 | tf_op jit(solution)/shard_map/psum | solution.py:59
  240.5 1.6 fusion.5
  242.4 3.7 collective-permute-done.4
  246.1 1.7 select_maximum_fusion.10
  247.8 52.0 %all-reduce.29.cloned.1.call-done = f32[4,4,32,256]{3,0,2,1:T(4,128)} async-done(((f32[4,4,32,256]{3,0,2,1:T(4,128)}), f32[4,4,32,256]{3,0,2,1:T(4,128)}) %all-reduce.29.cloned.1.call-update) | async-done | bytes 524304 | tf_op jit(solution)/shard_map/psum | solution.py:46
  301.9 4.7 fusion.136
  306.7 40.4 %all-reduce.9 = (f32[4]{0:T(128)S(1)}, f32[4]{0:T(128)S(1)}) all-reduce(f32[4]{0:T(128)} %get-tuple-element.9, f32[4]{0:T(128)} %get-tuple-element.8), channel_id=1, replica_groups=mesh['slab'=16,'grp'=8] {'slab'}, use_global_device_ids=true, to_apply=%region_15.16 | all-reduce | flops 8 | bytes 64 | tf_op jit(solution)/shard_map/psum | solution.py:59
  352.3 1.6 fusion.3
  354.0 4.1 collective-permute-done.6
  358.0 1.7 select_maximum_fusion.8
  359.8 51.8 %all-reduce.31.cloned.1.call-done = f32[4,4,32,256]{3,0,2,1:T(4,128)} async-done(((f32[4,4,32,256]{3,0,2,1:T(4,128)}), f32[4,4,32,256]{3,0,2,1:T(4,128)}) %all-reduce.31.cloned.1.call-update) | async-done | bytes 524304 | tf_op jit(solution)/shard_map/psum | solution.py:46
  411.6 1.4 reduce_sum.205
  413.6 5.5 fusion.137
  419.2 40.4 %all-reduce.8 = (f32[4]{0:T(128)S(1)}, f32[4]{0:T(128)S(1)}) all-reduce(f32[4]{0:T(128)} %get-tuple-element.7, f32[4]{0:T(128)} %get-tuple-element.6), channel_id=1, replica_groups=mesh['slab'=16,'grp'=8] {'slab'}, use_global_device_ids=true, to_apply=%region_21.22 | all-reduce | flops 8 | bytes 64 | tf_op jit(solution)/shard_map/psum | solution.py:59
  459.7 3.1 fusion.126
  462.8 35.5 %psum.194 = f32[4]{0:T(128)S(1)} all-reduce(f32[4]{0:T(128)S(1)} %get-tuple-element.48), channel_id=1, replica_groups=mesh['slab'=16,'grp'=8] {'slab'}, use_global_device_ids=true, to_apply=%region_25.26 | all-reduce | flops 4 | bytes 32 | tf_op jit(solution)/shard_map/psum | solution.py:88
  498.3 3.3 subtract_reduce_fusion.3
  502.3 4.5 collective-permute-start.9
  508.1 2.0 fusion.87
  511.3 3.6 convolution_bitcast_fusion.3
  515.8 2.7 select_maximum_fusion.6
  518.6 50.4 %all-reduce.39.cloned.1.call-done = (f32[4,4,32,256]{3,0,2,1:T(4,128)}, f32[4,32,256]{2,1,0:T(8,128)}) async-done(((f32[4,4,32,256]{3,0,2,1:T(4,128)}, f32[4,32,256]{2,1,0:T(8,128)}), (f32[4,4,32,256]{3,0,2,1:T(4,128)}, f32[4,32,256]{2,1,0:T(8,128)})) %all-reduce.39.cloned.1.call-update) | async-done | bytes 655376 | tf_op jit(solution)/shard_map/psum | solution.py:118
  569.0 6.2 fusion.127
  575.2 40.4 %psum.197 = f32[4]{0:T(128)S(1)} all-reduce(f32[4]{0:T(128)} %get-tuple-element.99), channel_id=1, replica_groups=mesh['slab'=16,'grp'=8] {'slab'}, use_global_device_ids=true, to_apply=%region_30.31 | all-reduce | flops 4 | bytes 32 | tf_op jit(solution)/shard_map/psum | solution.py:88
  616.2 3.0 subtract_reduce_fusion.2
  620.0 1.9 collective-permute-start.11
  623.2 2.0 fusion.84
  625.3 2.5 convolution_bitcast_fusion.2
  627.9 1.6 convolution_add_fusion.2
  629.5 2.7 select_maximum_fusion.4
  632.2 51.4 %all-reduce.37.cloned.1.call-done = (f32[4,4,32,256]{3,0,2,1:T(4,128)}, f32[4,32,256]{2,1,0:T(8,128)}) async-done(((f32[4,4,32,256]{3,0,2,1:T(4,128)}, f32[4,32,256]{2,1,0:T(8,128)}), (f32[4,4,32,256]{3,0,2,1:T(4,128)}, f32[4,32,256]{2,1,0:T(8,128)})) %all-reduce.37.cloned.1.call-update) | async-done | bytes 655376 | tf_op jit(solution)/shard_map/psum | solution.py:118
  683.6 5.9 fusion.128
  689.5 40.8 %psum.200 = f32[4]{0:T(128)S(1)} all-reduce(f32[4]{0:T(128)} %get-tuple-element.101), channel_id=1, replica_groups=mesh['slab'=16,'grp'=8] {'slab'}, use_global_device_ids=true, to_apply=%region_35.36 | all-reduce | flops 4 | bytes 32 | tf_op jit(solution)/shard_map/psum | solution.py:88
  731.0 2.9 subtract_reduce_fusion.1
  737.1 2.0 fusion.81
  739.3 2.5 convolution_bitcast_fusion.1
  741.8 1.6 convolution_add_fusion.1
  743.4 1.7 select_maximum_fusion.2
  745.2 52.4 %all-reduce.35.cloned.1.call-done = (f32[4,4,32,256]{3,0,2,1:T(4,128)}, f32[4,32,256]{2,1,0:T(8,128)}) async-done(((f32[4,4,32,256]{3,0,2,1:T(4,128)}, f32[4,32,256]{2,1,0:T(8,128)}), (f32[4,4,32,256]{3,0,2,1:T(4,128)}, f32[4,32,256]{2,1,0:T(8,128)})) %all-reduce.35.cloned.1.call-update) | async-done | bytes 655376 | tf_op jit(solution)/shard_map/psum | solution.py:118
  797.6 5.9 fusion.129
  803.5 40.4 %psum.203 = f32[4]{0:T(128)S(1)} all-reduce(f32[4]{0:T(128)} %get-tuple-element.103), channel_id=1, replica_groups=mesh['slab'=16,'grp'=8] {'slab'}, use_global_device_ids=true, to_apply=%region_40.41 | all-reduce | flops 4 | bytes 32 | tf_op jit(solution)/shard_map/psum | solution.py:88
  844.6 3.0 subtract_reduce_fusion
  847.7 2.5 convolution_bitcast_fusion
  850.4 12.4 %psum.206 = f32[4,4]{1,0:T(4,128)S(1)} all-reduce(f32[4,4]{1,0:T(4,128)S(1)} %convolution_add_fusion), channel_id=1, replica_groups=mesh['slab'=16,'grp'=8] {'grp'}, use_global_device_ids=true, to_apply=%region_44.45 | all-reduce | flops 16 | bytes 128 | tf_op jit(solution)/shard_map/psum | solution.py:159
  862.9 2.0 fusion.78
  864.9 35.4 %psum.207 = f32[4,4]{1,0:T(4,128)S(1)} all-reduce(f32[4,4]{1,0:T(4,128)S(1)} %psum.206), channel_id=1, replica_groups=mesh['slab'=16,'grp'=8] {'slab'}, use_global_device_ids=true, to_apply=%region_45.46 | all-reduce | flops 16 | bytes 128 | tf_op jit(solution)/shard_map/psum | solution.py:159
  900.4 3.9 collective-permute-start.15
  904.3 1.5 collective-permute-start.14
  906.8 4.4 collective-permute-done.14
  911.8 51.9 %all-reduce.33.cloned.1.call-done = (f32[4,4,32,256]{3,0,2,1:T(4,128)}, f32[4,32,256]{2,1,0:T(8,128)}) async-done(((f32[4,4,32,256]{3,0,2,1:T(4,128)}, f32[4,32,256]{2,1,0:T(8,128)}), (f32[4,4,32,256]{3,0,2,1:T(4,128)}, f32[4,32,256]{2,1,0:T(8,128)})) %all-reduce.33.cloned.1.call-update) | async-done | bytes 655376 | tf_op jit(solution)/shard_map/psum | solution.py:118
  963.8 3.0 fusion.20
  (176 shorter events, 37.7 us)
Async XLA Ops:
  7.2 10.7 %copy-start = (f32[4,4]{1,0:T(4,128)S(1)}, f32[4,4]{1,0:T(4,128)}, u32[]{:S(2)}) copy-start(f32[4,4]{1,0:T(4,128)} %param.9) | copy-start | bytes 196
  7.2 6.5 copy-start.1
  7.2 6.5 copy-start.39
  7.2 73.3 %all-reduce.25.cloned.1.call-start = ((), (), s32[]{:S(2)}) async-start(), calls=%async_computation | async-start | bytes 1048576 | tf_op jit(solution)/shard_map/psum | solution.py:46
  8.7 6.9 copy-start.38
  8.7 9.4 collective-permute-start.1
  12.4 6.9 collective-permute-start
  15.5 174.8 %all-reduce.27.cloned.1.call-start = ((), (), s32[]{:S(2)}) async-start(), calls=%async_computation.1 | async-start | bytes 1048576 | tf_op jit(solution)/shard_map/psum | solution.py:46
  17.1 219.8 %copy-start.22 = (f32[4,32,256]{2,1,0:T(8,128)}, f32[4,32,256]{2,1,0:T(8,128)S(1)}, u32[]{:S(2)}) copy-start(f32[4,32,256]{2,1,0:T(8,128)S(1)} %convert_element_type.23) | copy-start | bytes 393220
  17.2 110.5 %copy-start.20 = (f32[4,32,256]{2,1,0:T(8,128)}, f32[4,32,256]{2,1,0:T(8,128)S(1)}, u32[]{:S(2)}) copy-start(f32[4,32,256]{2,1,0:T(8,128)S(1)} %convert_element_type.22) | copy-start | bytes 393220
  81.9 4.9 copy-start.27
  86.8 41.6 %copy-start.5 = (f32[4,4,32,256]{3,0,2,1:T(4,128)}, f32[4,4,32,256]{3,0,2,1:T(4,128)S(1)}, u32[]{:S(2)}) copy-start(f32[4,4,32,256]{3,0,2,1:T(4,128)S(1)} %get-tuple-element.56) | copy-start | bytes 1572868
  86.8 41.6 %copy-start.7 = (f32[4,4,32,256]{3,0,2,1:T(4,128)}, f32[4,4,32,256]{3,0,2,1:T(4,128)S(1)}, u32[]{:S(2)}) copy-start(f32[4,4,32,256]{3,0,2,1:T(4,128)S(1)} %get-tuple-element.95) | copy-start | bytes 1572868
  128.4 4.3 collective-permute-start.3
  129.7 6.9 collective-permute-start.2
  132.6 167.2 %all-reduce.29.cloned.1.call-start = ((), (), s32[]{:S(2)}) async-start(), calls=%async_computation.2 | async-start | bytes 1048576 | tf_op jit(solution)/shard_map/psum | solution.py:46
  191.7 4.9 copy-start.31
  196.6 41.3 %copy-start.10 = (f32[4,4,32,256]{3,0,2,1:T(4,128)}, f32[4,4,32,256]{3,0,2,1:T(4,128)S(1)}, u32[]{:S(2)}) copy-start(f32[4,4,32,256]{3,0,2,1:T(4,128)S(1)} %get-tuple-element.55) | copy-start | bytes 1572868
  196.6 41.3 %copy-start.12 = (f32[4,4,32,256]{3,0,2,1:T(4,128)}, f32[4,4,32,256]{3,0,2,1:T(4,128)S(1)}, u32[]{:S(2)}) copy-start(f32[4,4,32,256]{3,0,2,1:T(4,128)S(1)} %get-tuple-element.96) | copy-start | bytes 1572868
  237.9 4.5 collective-permute-start.5
  239.2 6.9 collective-permute-start.4
  242.2 59.8 %copy-start.23 = (f32[4,32,256]{2,1,0:T(8,128)S(1)}, f32[4,32,256]{2,1,0:T(8,128)}, u32[]{:S(2)}) copy-start(f32[4,32,256]{2,1,0:T(8,128)} %convert_element_type.24) | copy-start | bytes 393220
  242.2 169.4 %all-reduce.31.cloned.1.call-start = ((), (), s32[]{:S(2)}) async-start(), calls=%async_computation.3 | async-start | bytes 1048576 | tf_op jit(solution)/shard_map/psum | solution.py:46
  301.2 5.5 copy-start.33
  306.7 43.0 %copy-start.15 = (f32[4,4,32,256]{3,0,2,1:T(4,128)}, f32[4,4,32,256]{3,0,2,1:T(4,128)S(1)}, u32[]{:S(2)}) copy-start(f32[4,4,32,256]{3,0,2,1:T(4,128)S(1)} %get-tuple-element.54) | copy-start | bytes 1572868
  306.7 43.0 %copy-start.17 = (f32[4,4,32,256]{3,0,2,1:T(4,128)}, f32[4,4,32,256]{3,0,2,1:T(4,128)S(1)}, u32[]{:S(2)}) copy-start(f32[4,4,32,256]{3,0,2,1:T(4,128)S(1)} %get-tuple-element.97) | copy-start | bytes 1572868
  349.7 4.3 collective-permute-start.7
  351.0 7.1 collective-permute-start.6
  353.9 59.7 %copy-start.24 = (f32[4,32,256]{2,1,0:T(8,128)S(1)}, f32[4,32,256]{2,1,0:T(8,128)}, u32[]{:S(2)}) copy-start(f32[4,32,256]{2,1,0:T(8,128)} %convert_element_type.25) | copy-start | bytes 393220
  353.9 215.1 %all-reduce.39.cloned.1.call-start = ((), (), s32[]{:S(2)}) async-start(), calls=%async_computation.7 | async-start | bytes 1310720 | tf_op jit(solution)/shard_map/psum | solution.py:118
  354.0 57.6 %copy-start.36 = (f32[4,1,32,256]{3,0,2,1:T(4,128)}, f32[4,1,32,256]{3,0,2,1:T(4,128)S(1)}, u32[]{:S(2)}) copy-start(f32[4,1,32,256]{3,0,2,1:T(4,128)S(1)} %collective-permute-done.7) | copy-start | bytes 393220
  358.0 54.9 %copy-start.37 = (f32[4,1,32,256]{3,0,2,1:T(4,128)}, f32[4,1,32,256]{3,0,2,1:T(4,128)S(1)}, u32[]{:S(2)}) copy-start(f32[4,1,32,256]{3,0,2,1:T(4,128)S(1)} %collective-permute-done.6) | copy-start | bytes 393220
  412.9 6.2 copy-start.34
  413.6 46.0 %copy-start.2 = (f32[4,32,256]{2,1,0:T(8,128)}, f32[4,32,256]{2,1,0:T(8,128)S(1)}, u32[]{:S(2)}) copy-start(f32[4,32,256]{2,1,0:T(8,128)S(1)} %get-tuple-element.80) | copy-start | bytes 393220
  413.6 46.0 %copy-start.25 = (f32[4,32,256]{2,1,0:T(8,128)S(1)}, f32[4,32,256]{2,1,0:T(8,128)}, u32[]{:S(2)}) copy-start(f32[4,32,256]{2,1,0:T(8,128)} %get-tuple-element.51) | copy-start | bytes 393220
  419.2 43.6 %copy-start.19 = (f32[4,4,32,256]{3,0,2,1:T(4,128)}, f32[4,4,32,256]{3,0,2,1:T(4,128)S(1)}, u32[]{:S(2)}) copy-start(f32[4,4,32,256]{3,0,2,1:T(4,128)S(1)} %get-tuple-element.53) | copy-start | bytes 1572868
  498.3 9.8 %copy-start.3 = (f32[4,32,256]{2,1,0:T(8,128)S(1)}, f32[4,32,256]{2,1,0:T(8,128)}, u32[]{:S(2)}) copy-start(f32[4,32,256]{2,1,0:T(8,128)} %copy-done.2) | copy-start | bytes 393220
  501.6 8.6 copy-start.18
  502.3 13.6 %collective-permute-start.9 = (f32[4,1,32,256]{3,0,2,1:T(4,128)}, f32[4,1,32,256]{3,0,2,1:T(4,128)}, u32[]{:S(2)}, u32[]{:S(2)}) collective-permute-start(f32[4,1,32,256]{3,0,2,1:T(4,128)} %get-tuple-element.63), channel_id=1, source_target_pairs={{0,8},{8,16},{16,24},{24,32},{32,40},{40,48},{48,56},{56,64},{64,7... | collective-permute-start | bytes 393224 | tf_op jit(solution)/shard_map/ppermute | solution.py:20
  506.8 9.0 collective-permute-start.8
  511.1 172.5 %all-reduce.37.cloned.1.call-start = ((), (), s32[]{:S(2)}) async-start(), calls=%async_computation.6 | async-start | bytes 1310720 | tf_op jit(solution)/shard_map/psum | solution.py:118
  569.0 47.3 %copy-start.16 = (f32[4,4,32,256]{3,0,2,1:T(4,128)S(1)}, f32[4,4,32,256]{3,0,2,1:T(4,128)}, u32[]{:S(2)}) copy-start(f32[4,4,32,256]{3,0,2,1:T(4,128)} %copy-done.15) | copy-start | bytes 1572868
  619.3 6.1 copy-start.14
  620.0 9.5 collective-permute-start.11
  621.9 7.5 collective-permute-start.10
  625.3 172.3 %all-reduce.35.cloned.1.call-start = ((), (), s32[]{:S(2)}) async-start(), calls=%async_computation.5 | async-start | bytes 1310720 | tf_op jit(solution)/shard_map/psum | solution.py:118
  627.9 55.7 %copy-start.13 = (f32[4,4,32,256]{3,0,2,1:T(4,128)S(1)}, f32[4,4,32,256]{3,0,2,1:T(4,128)}, u32[]{:S(2)}) copy-start(f32[4,4,32,256]{3,0,2,1:T(4,128)} %copy-done.12) | copy-start | bytes 1572868
  627.9 55.7 %copy-start.30 = (f32[4,32,256]{2,1,0:T(8,128)S(1)}, f32[4,32,256]{2,1,0:T(8,128)}, u32[]{:S(2)}) copy-start(f32[4,32,256]{2,1,0:T(8,128)} %get-tuple-element.81) | copy-start | bytes 393220
  683.6 47.4 %copy-start.11 = (f32[4,4,32,256]{3,0,2,1:T(4,128)S(1)}, f32[4,4,32,256]{3,0,2,1:T(4,128)}, u32[]{:S(2)}) copy-start(f32[4,4,32,256]{3,0,2,1:T(4,128)} %copy-done.10) | copy-start | bytes 1572868
  733.9 5.4 copy-start.9
  734.5 8.9 collective-permute-start.13
  735.8 7.6 collective-permute-start.12
  739.2 224.5 %all-reduce.33.cloned.1.call-start = ((), (), s32[]{:S(2)}) async-start(), calls=%async_computation.4 | async-start | bytes 1310720 | tf_op jit(solution)/shard_map/psum | solution.py:118
  741.8 55.8 %copy-start.8 = (f32[4,4,32,256]{3,0,2,1:T(4,128)S(1)}, f32[4,4,32,256]{3,0,2,1:T(4,128)}, u32[]{:S(2)}) copy-start(f32[4,4,32,256]{3,0,2,1:T(4,128)} %copy-done.7) | copy-start | bytes 1572868
  741.8 55.8 %copy-start.29 = (f32[4,32,256]{2,1,0:T(8,128)S(1)}, f32[4,32,256]{2,1,0:T(8,128)}, u32[]{:S(2)}) copy-start(f32[4,32,256]{2,1,0:T(8,128)} %get-tuple-element.83) | copy-start | bytes 393220
  741.8 55.8 %copy-start.32 = (f32[4,32,256]{2,1,0:T(8,128)S(1)}, f32[4,32,256]{2,1,0:T(8,128)}, u32[]{:S(2)}) copy-start(f32[4,32,256]{2,1,0:T(8,128)} %copy-done.31) | copy-start | bytes 393220
  797.6 47.0 %copy-start.6 = (f32[4,4,32,256]{3,0,2,1:T(4,128)S(1)}, f32[4,4,32,256]{3,0,2,1:T(4,128)}, u32[]{:S(2)}) copy-start(f32[4,4,32,256]{3,0,2,1:T(4,128)} %copy-done.5) | copy-start | bytes 1572868
  797.6 47.0 %copy-start.21 = (f32[4,32,256]{2,1,0:T(8,128)S(1)}, f32[4,32,256]{2,1,0:T(8,128)}, u32[]{:S(2)}) copy-start(f32[4,32,256]{2,1,0:T(8,128)} %copy-done.20) | copy-start | bytes 393220
  797.6 47.0 %copy-start.26 = (f32[4,32,256]{2,1,0:T(8,128)S(1)}, f32[4,32,256]{2,1,0:T(8,128)}, u32[]{:S(2)}) copy-start(f32[4,32,256]{2,1,0:T(8,128)} %get-tuple-element.73) | copy-start | bytes 393220
  844.6 5.6 copy-start.49
  900.4 6.4 collective-permute-start.15
  904.3 6.9 collective-permute-start.14
  905.8 58.0 %copy-start.28 = (f32[4,32,256]{2,1,0:T(8,128)S(1)}, f32[4,32,256]{2,1,0:T(8,128)}, u32[]{:S(2)}) copy-start(f32[4,32,256]{2,1,0:T(8,128)} %copy-done.27) | copy-start | bytes 393220
  905.8 58.0 %copy-start.35 = (f32[4,4,32,256]{3,0,2,1:T(4,128)S(1)}, f32[4,4,32,256]{3,0,2,1:T(4,128)}, u32[]{:S(2)}) copy-start(f32[4,4,32,256]{3,0,2,1:T(4,128)} %get-tuple-element.104) | copy-start | bytes 1572868
  (10 other events, 12.6 us)
Sparse Core Ops, SparseCore 0:
  15.7 64.7 all-reduce.24
  132.7 57.5 all-reduce.26
  242.3 57.5 all-reduce.28
  354.0 57.5 all-reduce.30
  511.2 57.7 all-reduce.38
  625.4 58.1 all-reduce.36
  739.3 58.1 all-reduce.34
  905.9 57.7 all-reduce.32
